TPU v7x, 32 devices: a whole 2x2x4 slice. The times are simulated.
32 devices in a mesh: groups: 2 (over x), blk: 8 (over z, y), rows: 2 (over core).
Axes of the slice: x: 2, y: 2, z: 4, core: 2. Of those that a mesh axis runs over, the one named last changes fastest.
Arguments:
- queries: bfloat16 [256, 2048], P(('groups', 'blk'), 'rows'), parts along dimension 0, may hold values from -170 to 170
- cache_keys: bfloat16 [8192, 256], P(('groups', 'blk'), 'rows'), parts along dimension 0, may hold values from -6 to 6
- cache_values: bfloat16 [8192, 256], P(('groups', 'blk'), 'rows'), parts along dimension 0, may hold values from -6 to 6
- span_starts: int32 [4], P('groups'), parts along dimension 0, may hold values from 0 to 4032, as said below
- out_weight: bfloat16 [2048, 2048], P(('rows', 'blk')), may hold values from -0.125 to 0.125
- norm_gain: bfloat16 [2048], replicated, may hold values from 0.099609375 to 1.8984375
- expert_ids: int32 [256, 8], P(('groups', 'blk', 'rows')), parts along dimension 0, may hold values from 0 to 15, all different within a row; in each aligned block of 8 rows (0 to 7, 8 to 15, ...) at most 8 rows name the same one
- gate_fixed: int32 [256, 8], P(('groups', 'blk', 'rows')), parts along dimension 0, may hold values from 1 to 4095
- gate_weight: bfloat16 [16, 2048, 768], P(('blk', 'rows')), may hold values from -0.125 to 0.125
- up_weight: bfloat16 [16, 2048, 768], P(('blk', 'rows')), may hold values from -0.125 to 0.125
- down_weight: bfloat16 [16, 768, 2048], P(('blk', 'rows')), may hold values from -0.21875 to 0.21875
Outputs:
- attn_proj: bfloat16 [256, 2048], P(('groups', 'blk', 'rows')), parts along dimension 0
- expert_out: bfloat16 [256, 2048], P(('groups', 'blk', 'rows')), parts along dimension 0
There are 2 independent parts, one for each index of `groups`. A program takes and returns all parts, laid end to end along the dimension named above; an argument that names none is the same for every part. Nothing has to cross between parts.
Inputs may be any that keep to these rules, and one draw needn't show every extreme that they name: `span_starts`: the last span ends at the last cached position, entry 1 is 4032; entry 0 is at most 3968. `expert_ids`: each token names 8 different experts; among the tokens of one device (aligned blocks of 8 rows) no expert is named more than 8 times.
All inputs are finite; a program needn't handle non-finite values.
Results may differ from a plain program's by a relative error of at most 0.035.
Values may be sent and summed in bfloat16 or wider, within the bound.
No kernel may reach another device: no remote copies, remote signals or barrier semaphores. Data moves between devices by JAX's collectives and lax.ppermute only.
A program may use at most 64 MiB of HBM per device.

v0:
```python
import math
import jax
import jax.numpy as jnp
from jax import lax
from jax.sharding import PartitionSpec as P

HD = 128
SPANS = 2
NEG_FILL = -1e30
EPSILON = 1e-06


def partial_attention(query_block, query_pos, cache_keys, cache_values, key_pos):
    rows_here = query_block.shape[0]
    kv_local = cache_keys.shape[1] // HD
    group_size = query_block.shape[1] // (kv_local * HD)
    heads_here = kv_local * group_size
    shaped_q = query_block.reshape(rows_here, kv_local, group_size, HD)
    shaped_k = cache_keys.reshape(-1, kv_local, HD)
    shaped_v = cache_values.reshape(-1, kv_local, HD)
    scores = jnp.einsum(
        "qgjd,kgd->qgjk", shaped_q, shaped_k, preferred_element_type=jnp.float32
    ) * (1.0 / math.sqrt(HD))
    visible = (key_pos[None, :] <= query_pos[:, None])[:, None, None, :]
    scores = jnp.where(visible, scores, NEG_FILL)
    row_top = jnp.max(scores, axis=-1)
    weights = jnp.where(visible, jnp.exp(scores - row_top[..., None]), 0.0)
    totals = jnp.sum(weights, axis=-1)
    numerator = jnp.einsum(
        "qgjk,kgd->qgjd", weights.astype(jnp.bfloat16), shaped_v, preferred_element_type=jnp.float32
    )
    return (
        row_top.reshape(rows_here, heads_here),
        totals.reshape(rows_here, heads_here),
        numerator.reshape(rows_here, heads_here * HD),
    )


def run_experts(arrived, gate_weight, up_weight, down_weight):
    gate_part = jnp.einsum(
        "secd,edf->secf", arrived, gate_weight, preferred_element_type=jnp.float32
    )
    up_part = jnp.einsum("secd,edf->secf", arrived, up_weight, preferred_element_type=jnp.float32)
    hidden = (jax.nn.silu(gate_part) * up_part).astype(jnp.bfloat16)
    return jnp.einsum(
        "secf,efd->secd", hidden, down_weight, preferred_element_type=jnp.float32
    ).astype(jnp.bfloat16)


def on_device(
    queries,
    cache_keys,
    cache_values,
    span_starts,
    out_weight,
    norm_gain,
    expert_ids,
    gate_fixed,
    gate_weight,
    up_weight,
    down_weight,
):
    gathered = lax.all_gather(queries, "blk", axis=0, tiled=True)
    total_rows = gathered.shape[0]
    width = gathered.shape[1]
    span_length = total_rows // SPANS
    token_index = jnp.arange(total_rows, dtype=jnp.int32)
    span_index = token_index // span_length
    span_match = span_index[:, None] == jnp.arange(SPANS, dtype=jnp.int32)[None, :]
    start_of = jnp.sum(jnp.where(span_match, span_starts[None, :], 0), axis=1)
    query_pos = start_of + token_index % span_length
    cache_rows = cache_keys.shape[0]
    key_pos = lax.axis_index("blk") * cache_rows + jnp.arange(cache_rows, dtype=jnp.int32)
    block_rows = math.gcd(total_rows, 128)
    block_count = total_rows // block_rows

    def one_block(item):
        return partial_attention(item[0], item[1], cache_keys, cache_values, key_pos)

    blocked = (
        gathered.reshape(block_count, block_rows, width),
        query_pos.reshape(block_count, block_rows),
    )
    row_top, totals, numerator = lax.map(one_block, blocked)
    heads_here = row_top.shape[2]
    row_top = row_top.reshape(total_rows, heads_here)
    totals = totals.reshape(total_rows, heads_here)
    numerator = numerator.reshape(total_rows, heads_here * HD)
    global_top = lax.pmax(row_top, "blk")
    factor = jnp.exp(row_top - global_top)
    totals = totals * factor
    numerator = (numerator.reshape(total_rows, heads_here, HD) * factor[:, :, None]).reshape(
        total_rows, heads_here * HD
    )
    own_numer = lax.psum_scatter(
        numerator.astype(jnp.bfloat16), "blk", scatter_dimension=1, tiled=True
    ).astype(jnp.float32)
    all_totals = lax.psum(totals, "blk")
    col_width = own_numer.shape[1]
    first_col = lax.axis_index("blk") * col_width
    spread = jnp.repeat(all_totals, HD, axis=1)
    col_totals = lax.dynamic_slice_in_dim(spread, first_col, col_width, 1)
    attended = (own_numer / col_totals).astype(jnp.bfloat16)
    projected = lax.psum_scatter(
        jnp.dot(attended, out_weight, preferred_element_type=jnp.float32),
        ("blk", "rows"),
        scatter_dimension=0,
        tiled=True,
    )
    attn_proj = projected.astype(jnp.bfloat16)
    values_f = attn_proj.astype(jnp.float32)
    mean_square = jnp.mean(values_f * values_f, axis=-1, keepdims=True)
    normed = (values_f * lax.rsqrt(mean_square + EPSILON) * norm_gain.astype(jnp.float32)).astype(
        jnp.bfloat16
    )
    own_tokens = normed.shape[0]
    top_count = expert_ids.shape[1]
    owners = lax.axis_size("blk") * lax.axis_size("rows")
    local_experts = gate_weight.shape[0]
    expert_count = owners * local_experts
    capacity = min(own_tokens, max(2, 2 * top_count * own_tokens // expert_count))
    slot_total = expert_count * capacity
    route_expert = expert_ids.reshape(-1)
    route_count = route_expert.shape[0]
    hits = (route_expert[:, None] == jnp.arange(expert_count, dtype=jnp.int32)[None, :]).astype(
        jnp.int32
    )
    slot_number = jnp.sum(jnp.cumsum(hits, axis=0) * hits, axis=1) - 1
    target = route_expert * capacity + slot_number
    placed = target[:, None] == jnp.arange(slot_total, dtype=jnp.int32)[None, :]
    route_token = jnp.arange(route_count, dtype=jnp.int32) // top_count
    token_pick = route_token[:, None] == jnp.arange(own_tokens, dtype=jnp.int32)[None, :]
    slot_token = jnp.dot(
        placed.astype(jnp.bfloat16).T,
        token_pick.astype(jnp.bfloat16),
        preferred_element_type=jnp.float32,
    ).astype(jnp.bfloat16)
    outgoing = jnp.dot(slot_token, normed, preferred_element_type=jnp.float32).astype(jnp.bfloat16)
    outgoing = outgoing.reshape(owners, local_experts, capacity, -1)
    gate_values = gate_fixed.astype(jnp.float32)
    route_weight = (gate_values / jnp.sum(gate_values, axis=1, keepdims=True)).reshape(-1)
    weighted_pick = token_pick.astype(jnp.float32) * route_weight[:, None]
    blend = jnp.dot(weighted_pick.T, placed.astype(jnp.float32), precision=lax.Precision.HIGHEST)
    finished = run_experts(
        lax.all_to_all(outgoing, ("blk", "rows"), split_axis=0, concat_axis=0, tiled=True),
        gate_weight,
        up_weight,
        down_weight,
    )
    returned = lax.all_to_all(finished, ("blk", "rows"), split_axis=0, concat_axis=0, tiled=True)
    returned_flat = returned.reshape(slot_total, -1)
    mixed = jnp.dot(blend, returned_flat.astype(jnp.float32), precision=lax.Precision.HIGHEST)
    expert_out = mixed.astype(jnp.bfloat16)
    return (attn_proj, expert_out)


def solution(mesh):
    in_specs = (
        P(("groups", "blk"), "rows"),
        P(("groups", "blk"), "rows"),
        P(("groups", "blk"), "rows"),
        P("groups"),
        P(("rows", "blk"), None),
        P(),
        P(("groups", "blk", "rows"), None),
        P(("groups", "blk", "rows"), None),
        P(("blk", "rows"), None, None),
        P(("blk", "rows"), None, None),
        P(("blk", "rows"), None, None),
    )
    out_specs = (P(("groups", "blk", "rows"), None), P(("groups", "blk", "rows"), None))
    return jax.shard_map(
        on_device, mesh=mesh, in_specs=in_specs, out_specs=out_specs, check_vma=False
    )
```

profile of v0, /device:TPU:0, one launch (start us, length us, event | category | flops | bytes accessed | tf_op | source)
XLA Modules:
  0.0 248.1 jit_solution(16907521409882701303)
XLA Ops:
  7.2 0.0 copy-start
  7.2 0.0 reduce-scatter.3.cloned.1.call-start
  7.3 0.9 fusion.69
  8.2 34.8 %all_gather.3 = bf16[128,1024]{1,0:T(8,128)(2,1)} all-gather(bf16[16,1024]{1,0:T(8,128)(2,1)} %param.11), channel_id=1, replica_groups=mesh['groups'=2,'blk'=8,'rows'=2] {'blk'}, dimensions={0}, use_global_device_ids=true | all-gather | bytes 294912 | tf_op jit(solution)/shard_map/all_gather | solution.py:63
  42.9 1.1 copy.25
  44.0 0.1 broadcast_compare_fusion
  44.2 2.7 %fusion.13 = (f32[128,8]{0,1:T(8,128)S(1)}, f32[512,128,8]{1,0,2:T(8,128)}) fusion(pred[128,512]{0,1:T(8,128)(4,1)S(1)} %broadcast_compare_fusion, bf16[128,8,128]{0,2,1:T(8,128)(2,1)S(1)} %bitcast.116, bf16[512,128]{1,0:T(8,128)(2,1)} %param.12), kind=kOutput, calls=%fused_computation.13 | convolution fusion | flops 135789568 | bytes 2560000 | tf_op jit(solution)/shard_map/while/body/eval_jaxpr/qgjd,kgd->qgjk/dot_general | solution.py:21
  46.9 21.3 %pmax.7 = f32[128,8]{0,1:T(8,128)S(1)} all-reduce(f32[128,8]{0,1:T(8,128)S(1)} %get-tuple-element.24), channel_id=1, replica_groups=mesh['groups'=2,'blk'=8,'rows'=2] {'blk'}, use_global_device_ids=true, to_apply=%region_2.3 | all-reduce | flops 1024 | bytes 8192 | tf_op jit(solution)/shard_map/pmax | solution.py:89
  68.2 0.0 copy-start.1
  68.2 2.2 fusion.14
  70.5 0.0 copy-done.1
  70.5 1.5 fusion.32
  72.0 0.0 copy-start.6
  72.0 0.0 copy-start.5
  72.1 0.7 fusion.37
  72.8 0.0 reduce-scatter.3.cloned.1.call-update
  72.8 0.0 reduce-scatter.5.cloned.1.call-start
  72.9 17.1 %psum.7 = f32[128,8]{0,1:T(8,128)S(1)} all-reduce(f32[128,8]{0,1:T(8,128)S(1)} %get-tuple-element.22), channel_id=1, replica_groups=mesh['groups'=2,'blk'=8,'rows'=2] {'blk'}, use_global_device_ids=true, to_apply=%region_5.6 | all-reduce | flops 1024 | bytes 8192 | tf_op jit(solution)/shard_map/psum | solution.py:98
  90.0 42.7 %reduce-scatter.3.cloned.1.call-done = bf16[128,128]{0,1:T(8,128)(2,1)} async-done(((bf16[128,1024]{0,1:T(8,128)(2,1)}), bf16[128,128]{0,1:T(8,128)(2,1)}) %reduce-scatter.3.cloned.1.call-update) | async-done | bytes 32784 | tf_op jit(solution)/shard_map/reduce_scatter | solution.py:95
  132.7 2.4 fusion.54
  135.1 0.0 reduce-scatter.5.cloned.1.call-update
  135.1 0.0 copy-done.6
  135.1 0.1 reshape.171
  135.2 0.1 fusion.59
  135.3 0.1 reduce_window_sum.11
  135.4 0.0 copy-done.5
  135.4 0.2 select_reduce_fusion
  135.6 57.3 %reduce-scatter.5.cloned.1.call-done = f32[8,2048]{1,0:T(8,128)} async-done(((f32[128,2048]{1,0:T(8,128)}), f32[8,2048]{1,0:T(8,128)}) %reduce-scatter.5.cloned.1.call-update) | async-done | bytes 65552 | tf_op jit(solution)/shard_map/reduce_scatter | solution.py:104
  192.9 1.0 fusion.51
  193.9 0.0 copy-start.3
  193.9 1.4 fusion.12
  195.3 0.0 copy-done.3
  195.3 18.0 %all_to_all.10 = bf16[16,1,8,2048]{3,2,1,0:T(8,128)(2,1)S(1)} all-to-all(bf16[16,1,8,2048]{3,2,1,0:T(8,128)(2,1)} %fusion.12), channel_id=1, replica_groups=mesh['groups'=2,'blk'=8,'rows'=2] {'blk','rows'}, dimensions={0} | all-to-all | bytes 1048576 | tf_op jit(solution)/shard_map/all_to_all | solution.py:145
  213.3 0.0 copy-start.2
  213.3 0.8 copy-done.2
  214.2 2.5 fusion.16
  216.6 0.0 copy-done
  216.6 0.0 copy-start.4
  216.7 4.1 %fusion.9 = bf16[16,1,8,2048]{3,2,1,0:T(8,128)(2,1)} fusion(bf16[1,768,2048]{2,1,0:T(8,128)(2,1)S(1)} %copy-done, bf16[1,2048,768]{2,1,0:T(8,128)(2,1)} %param.20, bf16[16,1,8,2048]{3,2,1,0:T(8,128)(2,1)} %copy-done.2, f32[16,1,8,768]{3,2,0,1:T(8,128)S(1)} %fusion.16), kind=kOutput, calls=%fused_computation.8 | convolution fusion | flops 806158336 | bytes 7733248 | tf_op jit(solution)/shard_map/secf,efd->secd/dot_general | solution.py:45
  220.7 4.2 %all-to-all-start.1 = ((bf16[16,1,8,2048]{3,2,1,0:T(8,128)(2,1)}), bf16[16,1,8,2048]{3,2,1,0:T(8,128)(2,1)}, u32[]{:S(2)}, u32[]{:S(2)}) async-start(bf16[16,1,8,2048]{3,2,1,0:T(8,128)(2,1)} %fusion.9), calls=%async_computation.3 | async-start | bytes 1048576 | tf_op jit(solution)/shard_map/all_to_all | solution.py:150
  225.0 0.0 copy-done.4
  225.0 0.1 convert_reduce_fusion
  225.1 0.1 convert_divide_fusion
  225.2 0.1 mul.86
  225.3 0.3 fusion.58
  225.5 13.8 %all-to-all-done.1 = bf16[16,1,8,2048]{3,2,1,0:T(8,128)(2,1)} async-done(((bf16[16,1,8,2048]{3,2,1,0:T(8,128)(2,1)}), bf16[16,1,8,2048]{3,2,1,0:T(8,128)(2,1)}, u32[]{:S(2)}, u32[]{:S(2)}) %all-to-all-start.1) | async-done | bytes 524320 | tf_op jit(solution)/shard_map/all_to_all | solution.py:150
  239.3 2.0 convolution_convert_fusion.1
  (8 shorter events, 0.1 us)
Async XLA Ops:
  7.2 209.5 %copy-start = (bf16[1,768,2048]{2,1,0:T(8,128)(2,1)S(1)}, bf16[1,768,2048]{2,1,0:T(8,128)(2,1)}, u32[]{:S(2)}) copy-start(bf16[1,768,2048]{2,1,0:T(8,128)(2,1)} %param.21) | copy-start | bytes 9437188
  7.2 125.5 %reduce-scatter.3.cloned.1.call-start = ((), (), s32[]{:S(2)}) async-start(), calls=%async_computation.4 | async-start | bytes 294912 | tf_op jit(solution)/shard_map/reduce_scatter | solution.py:95
  68.2 2.3 copy-start.1
  72.0 63.1 %copy-start.6 = (s32[8,8]{1,0:T(8,128)S(1)}, s32[8,8]{1,0:T(8,128)}, u32[]{:S(2)}) copy-start(s32[8,8]{1,0:T(8,128)} %param.17) | copy-start | bytes 772
  72.0 63.4 %copy-start.5 = (bf16[2048]{0:T(1024)(128)(2,1)S(1)}, bf16[2048]{0:T(1024)(128)(2,1)}, u32[]{:S(2)}) copy-start(bf16[2048]{0:T(1024)(128)(2,1)} %param.16) | copy-start | bytes 12292
  72.8 120.1 %reduce-scatter.5.cloned.1.call-start = ((), (), s32[]{:S(2)}) async-start(), calls=%async_computation.5 | async-start | bytes 1114112 | tf_op jit(solution)/shard_map/reduce_scatter | solution.py:104
  193.9 1.4 copy-start.3
  213.3 0.8 copy-start.2
  216.6 8.3 %copy-start.4 = (s32[8,8]{1,0:T(8,128)S(1)}, s32[8,8]{1,0:T(8,128)}, u32[]{:S(2)}) copy-start(s32[8,8]{1,0:T(8,128)} %param.18) | copy-start | bytes 772
  220.7 18.6 %all-to-all-start.1 = ((bf16[16,1,8,2048]{3,2,1,0:T(8,128)(2,1)}), bf16[16,1,8,2048]{3,2,1,0:T(8,128)(2,1)}, u32[]{:S(2)}, u32[]{:S(2)}) async-start(bf16[16,1,8,2048]{3,2,1,0:T(8,128)(2,1)} %fusion.9), calls=%async_computation.3 | async-start | bytes 1048576 | tf_op jit(solution)/shard_map/all_to_all | solution.py:150
Sparse Core Ops, SparseCore 0:
  72.9 59.7 reduce-scatter.2
  136.3 56.6 reduce-scatter.4
where the time goes:
time: 249 us; the launch traced here: 248 us
  waiting for transfers between devices  114 us (46%)
  blocking collectives  91.3 us (37%)
  matrix products  16.8 us (7%)
  between operations  14.2 us (6%)
  other arithmetic  5.54 us (2%)
  starting transfers between devices  4.32 us (2%)
    reduce_scatter x1, waiting for transfers between devices, on_device(): lax.psum_scatter(jnp.dot(attended, out_weight, preferred_element_type=jnp...  57.3 us
    reduce_scatter x1, waiting for transfers between devices, on_device(): lax.psum_scatter(numerator.astype(jnp.bfloat16), 'blk', scatter_dimension...  42.7 us
    all_gather x1, blocking collectives, on_device(): gathered = lax.all_gather(queries, 'blk', axis=0, tiled=True)  34.8 us
    pmax x1, blocking collectives, on_device(): global_top = lax.pmax(row_top, 'blk')  21.3 us
    all_to_all x1, blocking collectives, on_device(): lax.all_to_all(outgoing, ('blk', 'rows'), split_axis=0, concat_axis=0, ti...  18 us
    psum x1, blocking collectives, on_device(): all_totals = lax.psum(totals, 'blk')  17.1 us
    all_to_all x1, waiting for transfers between devices, on_device(): lax.all_to_all(finished, ('blk', 'rows'), split_axis=0, concat_axis=0, ti...  13.8 us
  transfers between devices with their start and end apart: 3, of which 3 were waited for; matrix products, arithmetic and copies ran while one was open for 0% of the time, Pallas kernels for 0%

commit v1 on v0

--- a/solution.py
+++ b/solution.py
@@ -60,7 +60,9 @@
     up_weight,
     down_weight,
 ):
-    gathered = lax.all_gather(queries, "blk", axis=0, tiled=True)
+    gathered = jnp.concatenate(
+        lax.all_to_all(jnp.stack([queries] * lax.axis_size("blk")), "blk", 0, 0), axis=0
+    )
     total_rows = gathered.shape[0]
     width = gathered.shape[1]
     span_length = total_rows // SPANS

time: 249 us -> 227 us (0.912)
  blocking collectives: 91.3 us -> 54.6 us
  waiting for transfers between devices: 114 us -> 122 us
  starting transfers between devices: 4.32 us -> 11.6 us
    all_gather x1 -> x0, blocking collectives: 34.8 us -> none  [on_device(): gathered = lax.all_gather(queries, 'blk', axis=0, tiled=True)]
    all_to_all x0 -> x1, waiting for transfers between devices: none -> 7.96 us  [on_device(): lax.all_to_all(jnp.stack([queries] * lax.axis_size('blk')), 'blk', 0, 0)]
    all_to_all x0 -> x1, starting transfers between devices: none -> 7.31 us  [on_device(): lax.all_to_all(jnp.stack([queries] * lax.axis_size('blk')), 'blk', 0, 0)]
  transfers between devices with their start and end apart: 3 -> 4, of which waited for: 3 -> 4; matrix products, arithmetic and copies ran while one was open for 0% -> 1% of each run, Pallas kernels for 0% -> 0%
where the time goes in v1:
time: 227 us; the launch traced here: 226 us
  waiting for transfers between devices  122 us (54%)
  blocking collectives  54.6 us (24%)
  matrix products  15.9 us (7%)
  between operations  14.2 us (6%)
  starting transfers between devices  11.6 us (5%)
  other arithmetic  5.38 us (2%)
  local copies, waits for them, and re-layouts  2.72 us (1%)
    reduce_scatter x1, waiting for transfers between devices, on_device(): lax.psum_scatter(jnp.dot(attended, out_weight, preferred_element_type=jnp...  57.4 us
    reduce_scatter x1, waiting for transfers between devices, on_device(): lax.psum_scatter(numerator.astype(jnp.bfloat16), 'blk', scatter_dimension...  42.7 us
    pmax x1, blocking collectives, on_device(): global_top = lax.pmax(row_top, 'blk')  19.4 us
    all_to_all x1, blocking collectives, on_device(): lax.all_to_all(outgoing, ('blk', 'rows'), split_axis=0, concat_axis=0, ti...  18.1 us
    psum x1, blocking collectives, on_device(): all_totals = lax.psum(totals, 'blk')  17.1 us
    all_to_all x1, waiting for transfers between devices, on_device(): lax.all_to_all(finished, ('blk', 'rows'), split_axis=0, concat_axis=0, ti...  13.8 us
    all_to_all x1, waiting for transfers between devices, on_device(): lax.all_to_all(jnp.stack([queries] * lax.axis_size('blk')), 'blk', 0, 0)  7.96 us
    all_to_all x1, starting transfers between devices, on_device(): lax.all_to_all(jnp.stack([queries] * lax.axis_size('blk')), 'blk', 0, 0)  7.31 us
  transfers between devices with their start and end apart: 4, of which 4 were waited for; matrix products, arithmetic and copies ran while one was open for 1% of the time, Pallas kernels for 0%

profile of v1, /device:TPU:0, one launch (start us, length us, event | category | flops | bytes accessed | tf_op | source)
XLA Modules:
  0.0 226.3 jit_solution(11438854006227389007)
XLA Ops:
  7.2 0.0 copy-start
  7.2 1.6 stack.2
  8.8 7.3 %all-to-all-start = ((bf16[8,16,1024]{2,1,0:T(8,128)(2,1)}), bf16[8,16,1024]{2,1,0:T(8,128)(2,1)S(1)}, u32[]{:S(2)}, u32[]{:S(2)}) async-start(bf16[8,16,1024]{2,1,0:T(8,128)(2,1)} %stack.2), calls=%async_computation | async-start | bytes 524288 | tf_op jit(solution)/shard_map/all_to_all | solution.py:64
  16.1 0.0 reduce-scatter.3.cloned.1.call-start
  16.2 0.7 fusion.70
  16.9 0.1 broadcast_compare_fusion
  17.1 8.0 %all-to-all-done = bf16[8,16,1024]{2,1,0:T(8,128)(2,1)S(1)} async-done(((bf16[8,16,1024]{2,1,0:T(8,128)(2,1)}), bf16[8,16,1024]{2,1,0:T(8,128)(2,1)S(1)}, u32[]{:S(2)}, u32[]{:S(2)}) %all-to-all-start) | async-done | bytes 262176 | tf_op jit(solution)/shard_map/all_to_all | solution.py:64
  25.1 0.0 copy-start.7
  25.1 2.7 %fusion.13 = (f32[128,8]{0,1:T(8,128)S(1)}, f32[512,128,8]{1,0,2:T(8,128)}) fusion(pred[128,512]{0,1:T(8,128)(4,1)S(1)} %broadcast_compare_fusion, bf16[128,8,128]{2,1,0:T(8,128)(2,1)S(1)} %bitcast.117, bf16[512,128]{1,0:T(8,128)(2,1)} %param.12), kind=kOutput, calls=%fused_computation.13 | convolution fusion | flops 135789568 | bytes 2560000 | tf_op jit(solution)/shard_map/while/body/eval_jaxpr/qgjd,kgd->qgjk/dot_general | solution.py:21
  27.8 19.4 %pmax.7 = f32[128,8]{0,1:T(8,128)S(1)} all-reduce(f32[128,8]{0,1:T(8,128)S(1)} %get-tuple-element.24), channel_id=1, replica_groups=mesh['groups'=2,'blk'=8,'rows'=2] {'blk'}, use_global_device_ids=true, to_apply=%region_2.3 | all-reduce | flops 1024 | bytes 8192 | tf_op jit(solution)/shard_map/pmax | solution.py:91
  47.2 0.0 copy-start.1
  47.2 2.2 fusion.14
  49.5 0.0 copy-done.7
  49.5 0.0 copy-done.1
  49.5 0.6 fusion.32
  50.2 0.0 copy-start.6
  50.2 0.0 copy-start.5
  50.2 0.7 fusion.37
  50.9 0.0 reduce-scatter.3.cloned.1.call-update
  50.9 0.0 reduce-scatter.5.cloned.1.call-start
  51.0 17.1 %psum.7 = f32[128,8]{0,1:T(8,128)S(1)} all-reduce(f32[128,8]{0,1:T(8,128)S(1)} %get-tuple-element.22), channel_id=1, replica_groups=mesh['groups'=2,'blk'=8,'rows'=2] {'blk'}, use_global_device_ids=true, to_apply=%region_5.6 | all-reduce | flops 1024 | bytes 8192 | tf_op jit(solution)/shard_map/psum | solution.py:100
  68.1 42.7 %reduce-scatter.3.cloned.1.call-done = bf16[128,128]{0,1:T(8,128)(2,1)} async-done(((bf16[128,1024]{0,1:T(8,128)(2,1)}), bf16[128,128]{0,1:T(8,128)(2,1)}) %reduce-scatter.3.cloned.1.call-update) | async-done | bytes 32784 | tf_op jit(solution)/shard_map/reduce_scatter | solution.py:97
  110.9 2.4 %fusion.55 = f32[128,2048]{1,0:T(8,128)} fusion(bf16[128,2048]{1,0:T(8,128)(2,1)} %param.15, f32[128,1024]{0,1:T(8,128)S(1)} %bitcast.119, s32[]{:T(128)S(6)} %select_n.48, bf16[128,128]{0,1:T(8,128)(2,1)} %reduce-scatter.3.cloned.1.call-done), kind=kOutput, calls=%fused_computation.47 | convolution fusion | flops 67158016 | bytes 1671172 | tf_op jit(solution)/shard_map/dot_general | solution.py:107
  113.3 0.0 reduce-scatter.5.cloned.1.call-update
  113.3 0.0 copy-done.6
  113.3 0.1 reshape.171
  113.4 0.1 fusion.60
  113.4 0.1 reduce_window_sum.11
  113.5 0.0 copy-done.5
  113.6 0.2 select_reduce_fusion
  113.7 57.4 %reduce-scatter.5.cloned.1.call-done = f32[8,2048]{1,0:T(8,128)} async-done(((f32[128,2048]{1,0:T(8,128)}), f32[8,2048]{1,0:T(8,128)}) %reduce-scatter.5.cloned.1.call-update) | async-done | bytes 65552 | tf_op jit(solution)/shard_map/reduce_scatter | solution.py:106
  171.1 1.0 fusion.52
  172.1 1.4 fusion.12
  173.5 0.0 copy-done.3
  173.5 18.1 %all_to_all.15 = bf16[16,1,8,2048]{3,2,1,0:T(8,128)(2,1)S(1)} all-to-all(bf16[16,1,8,2048]{3,2,1,0:T(8,128)(2,1)} %fusion.12), channel_id=1, replica_groups=mesh['groups'=2,'blk'=8,'rows'=2] {'blk','rows'}, dimensions={0} | all-to-all | bytes 1048576 | tf_op jit(solution)/shard_map/all_to_all | solution.py:147
  191.6 0.8 copy-done.2
  192.4 2.5 %fusion.16 = f32[16,1,8,768]{3,2,0,1:T(8,128)S(1)} fusion(bf16[1,2048,768]{2,1,0:T(8,128)(2,1)} %param.19, bf16[16,1,8,2048]{3,2,1,0:T(8,128)(2,1)S(1)} %all_to_all.15), kind=kOutput, calls=%fused_computation.16 | convolution fusion | flops 402653184 | bytes 4063232 | tf_op jit(solution)/shard_map/secd,edf->secf/dot_general | solution.py:40
  194.8 0.0 copy-done
  194.9 0.0 copy-start.4
  194.9 4.1 %fusion.9 = bf16[16,1,8,2048]{3,2,1,0:T(8,128)(2,1)} fusion(bf16[1,768,2048]{2,1,0:T(8,128)(2,1)S(1)} %copy-done, bf16[1,2048,768]{2,1,0:T(8,128)(2,1)} %param.20, bf16[16,1,8,2048]{3,2,1,0:T(8,128)(2,1)} %copy-done.2, f32[16,1,8,768]{3,2,0,1:T(8,128)S(1)} %fusion.16), kind=kOutput, calls=%fused_computation.8 | convolution fusion | flops 806158336 | bytes 7733248 | tf_op jit(solution)/shard_map/secf,efd->secd/dot_general | solution.py:45
  198.9 4.2 %all-to-all-start.2 = ((bf16[16,1,8,2048]{3,2,1,0:T(8,128)(2,1)}), bf16[16,1,8,2048]{3,2,1,0:T(8,128)(2,1)}, u32[]{:S(2)}, u32[]{:S(2)}) async-start(bf16[16,1,8,2048]{3,2,1,0:T(8,128)(2,1)} %fusion.9), calls=%async_computation.4 | async-start | bytes 1048576 | tf_op jit(solution)/shard_map/all_to_all | solution.py:152
  203.2 0.0 copy-done.4
  203.2 0.1 convert_reduce_fusion
  203.3 0.1 convert_divide_fusion
  203.4 0.1 mul.86
  203.5 0.3 fusion.59
  203.8 13.8 %all-to-all-done.2 = bf16[16,1,8,2048]{3,2,1,0:T(8,128)(2,1)} async-done(((bf16[16,1,8,2048]{3,2,1,0:T(8,128)(2,1)}), bf16[16,1,8,2048]{3,2,1,0:T(8,128)(2,1)}, u32[]{:S(2)}, u32[]{:S(2)}) %all-to-all-start.2) | async-done | bytes 524320 | tf_op jit(solution)/shard_map/all_to_all | solution.py:152
  217.5 2.0 convolution_convert_fusion.1
  (11 shorter events, 0.1 us)
Async XLA Ops:
  7.2 187.7 %copy-start = (bf16[1,768,2048]{2,1,0:T(8,128)(2,1)S(1)}, bf16[1,768,2048]{2,1,0:T(8,128)(2,1)}, u32[]{:S(2)}) copy-start(bf16[1,768,2048]{2,1,0:T(8,128)(2,1)} %param.21) | copy-start | bytes 9437188
  8.8 16.2 %all-to-all-start = ((bf16[8,16,1024]{2,1,0:T(8,128)(2,1)}), bf16[8,16,1024]{2,1,0:T(8,128)(2,1)S(1)}, u32[]{:S(2)}, u32[]{:S(2)}) async-start(bf16[8,16,1024]{2,1,0:T(8,128)(2,1)} %stack.2), calls=%async_computation | async-start | bytes 524288 | tf_op jit(solution)/shard_map/all_to_all | solution.py:64
  16.1 94.7 %reduce-scatter.3.cloned.1.call-start = ((), (), s32[]{:S(2)}) async-start(), calls=%async_computation.5 | async-start | bytes 294912 | tf_op jit(solution)/shard_map/reduce_scatter | solution.py:97
  25.1 24.4 %copy-start.7 = (bf16[512,128]{1,0:T(8,128)(2,1)S(1)}, bf16[512,128]{1,0:T(8,128)(2,1)}, u32[]{:S(2)}) copy-start(bf16[512,128]{1,0:T(8,128)(2,1)} %param.13) | copy-start | bytes 393220
  47.2 2.3 copy-start.1
  50.2 63.1 %copy-start.6 = (s32[8,8]{1,0:T(8,128)S(1)}, s32[8,8]{1,0:T(8,128)}, u32[]{:S(2)}) copy-start(s32[8,8]{1,0:T(8,128)} %param.17) | copy-start | bytes 772
  50.2 63.4 %copy-start.5 = (bf16[2048]{0:T(1024)(128)(2,1)S(1)}, bf16[2048]{0:T(1024)(128)(2,1)}, u32[]{:S(2)}) copy-start(bf16[2048]{0:T(1024)(128)(2,1)} %param.16) | copy-start | bytes 12292
  50.9 120.2 %reduce-scatter.5.cloned.1.call-start = ((), (), s32[]{:S(2)}) async-start(), calls=%async_computation.6 | async-start | bytes 1114112 | tf_op jit(solution)/shard_map/reduce_scatter | solution.py:106
  172.1 1.4 copy-start.3
  191.6 0.8 copy-start.2
  194.9 8.3 %copy-start.4 = (s32[8,8]{1,0:T(8,128)S(1)}, s32[8,8]{1,0:T(8,128)}, u32[]{:S(2)}) copy-start(s32[8,8]{1,0:T(8,128)} %param.18) | copy-start | bytes 772
  198.9 18.6 %all-to-all-start.2 = ((bf16[16,1,8,2048]{3,2,1,0:T(8,128)(2,1)}), bf16[16,1,8,2048]{3,2,1,0:T(8,128)(2,1)}, u32[]{:S(2)}, u32[]{:S(2)}) async-start(bf16[16,1,8,2048]{3,2,1,0:T(8,128)(2,1)} %fusion.9), calls=%async_computation.4 | async-start | bytes 1048576 | tf_op jit(solution)/shard_map/all_to_all | solution.py:152
Sparse Core Ops, SparseCore 0:
  51.1 59.7 reduce-scatter.2
  114.4 56.6 reduce-scatter.4
